TPU v7x, 32 devices: a whole 2x2x4 slice. The times are simulated.
32 devices in a mesh: groups: 2 (over y), rows: 4 (over z), tm: 4 (over x, core).
Axes of the slice: x: 2, y: 2, z: 4, core: 2. Of those that a mesh axis runs over, the one named last changes fastest.
Arguments:
- video: bfloat16 [2, 16, 8, 96, 128], P('groups', 'tm', 'rows'), parts along dimension 0, may hold values from -6 to 6
- gamma_first: float32 [96], replicated, may hold values from 0.25 to 1.75
- kernel_first: bfloat16 [96, 2592], replicated, may hold values from -0.125 to 0.125
- bias_first: float32 [96], replicated, may hold values from -3 to 3
- gamma_second: float32 [96], replicated, may hold values from 0.25 to 1.75
- kernel_second: bfloat16 [96, 2592], replicated, may hold values from -0.125 to 0.125
- bias_second: float32 [96], replicated, may hold values from -3 to 3
Outputs:
- encoded: bfloat16 [2, 16, 8, 96, 128], P('groups', 'tm', 'rows'), parts along dimension 0
There are 2 independent parts, one for each index of `groups`. A program takes and returns all parts, laid end to end along the dimension named above; an argument that names none is the same for every part. Nothing has to cross between parts.
All inputs are finite; a program needn't handle non-finite values.
Results may differ from a plain program's by a relative error of at most 0.0036.
Values may be sent and summed in bfloat16 or wider, within the bound.
A program may use at most 64 MiB of HBM per device.

v0:
```python
import jax
import jax.numpy as jnp
from jax import lax
from jax.sharding import PartitionSpec as P

epsilon = 1e-06


def passed_along(block, axis, distance):
    devices = range(lax.axis_size(axis))
    route = [(i - distance, i) for i in devices if i - distance in devices]
    return lax.ppermute(block, axis, route)


def padded_2(cells, sides, width):
    for axis, dim in sides:
        count = lax.axis_size(axis)
        ends = count - 1
        head = lax.slice_in_dim(cells, 0, width, axis=dim)
        tail = lax.slice_in_dim(cells, cells.shape[dim] - width, cells.shape[dim], axis=dim)
        cells = jnp.concatenate(
            [
                lax.ppermute(tail, axis, [(i, (i + 1) % count) for i in range(ends)]),
                cells,
                lax.ppermute(head, axis, [((i + 1) % count, i) for i in range(ends)]),
            ],
            axis=dim,
        )
    return cells


def norm_silu(values, gain):
    meansq = jnp.mean(values * values, axis=3, keepdims=True)
    scaled = values * lax.rsqrt(meansq + epsilon) * gain[:, None]
    return jax.nn.silu(scaled)


def conv_valid(extended, kernel, offset):
    chans = extended.shape[3]
    width = extended.shape[4]
    out_frames = extended.shape[1] - 2
    out_rows = extended.shape[2] - 2
    padded = jnp.pad(extended, ((0, 0), (0, 0), (0, 0), (0, 0), (1, 1)))
    summed = jnp.zeros((extended.shape[0], out_frames, out_rows, chans, width), jnp.float32)
    for frame_off in range(3):
        for row_off in range(3):
            section = padded[:, frame_off : frame_off + out_frames, row_off : row_off + out_rows]
            stacked = jnp.concatenate(
                [section[..., 0:width], section[..., 1 : width + 1], section[..., 2 : width + 2]],
                axis=3,
            )
            start = (frame_off * 3 + row_off) * 3 * chans
            columns = kernel[:, start : start + 3 * chans]
            summed = summed + jnp.einsum(
                "oc,bfrcw->bfrow", columns, stacked, preferred_element_type=jnp.float32
            )
    return summed + offset[:, None]


def local(video, gamma_first, kernel_first, bias_first, gamma_second, kernel_second, bias_second):
    frames = video.shape[1]
    tile_rows = video.shape[2]
    prior = passed_along(video, "tm", 1)
    joined = jnp.concatenate([prior, video], axis=1)
    margin = padded_2(joined, (("rows", 2),), 2)
    first = norm_silu(margin.astype(jnp.float32), gamma_first).astype(jnp.bfloat16)
    hidden = conv_valid(first, kernel_first, bias_first)
    second = norm_silu(hidden, gamma_second).astype(jnp.bfloat16)
    frame_pos = jnp.arange(frames + 2, dtype=jnp.int32) - 2 + lax.axis_index("tm") * frames
    row_pos = jnp.arange(tile_rows + 2, dtype=jnp.int32) - 1 + lax.axis_index("rows") * tile_rows
    row_limit = tile_rows * lax.axis_size("rows")
    inside = (frame_pos >= 0)[:, None] & ((row_pos >= 0) & (row_pos < row_limit))[None, :]
    second = jnp.where(inside[None, :, :, None, None], second, jnp.zeros_like(second))
    result = conv_valid(second, kernel_second, bias_second)
    return (video.astype(jnp.float32) + result).astype(jnp.bfloat16)


def solution(mesh):
    in_specs = (P("groups", "tm", "rows", None, None), P(), P(), P(), P(), P(), P())
    out_specs = P("groups", "tm", "rows", None, None)
    return jax.shard_map(local, mesh=mesh, in_specs=in_specs, out_specs=out_specs, check_vma=False)
```

profile of v0, /device:TPU:1, one launch (start us, length us, event | category | flops | bytes accessed | tf_op | source)
XLA Modules:
  0.0 39.6 jit_solution(17630420195884164558)
XLA Ops:
  0.0 4.6 %collective-permute-start = (bf16[1,4,2,96,128]{4,3,2,1,0:T(8,128)(2,1)}, bf16[1,4,2,96,128]{4,3,2,1,0:T(8,128)(2,1)S(1)}, u32[]{:S(2)}, u32[]{:S(2)}) collective-permute-start(bf16[1,4,2,96,128]{4,3,2,1,0:T(8,128)(2,1)} %param.7), channel_id=1, source_target_pairs={{0,1},{1,2},{2,3},{4,5},{5,6},{6,7},{8,9},{9,10},{10,11},{12,13},{... | collective-permute-start | bytes 589832 | tf_op jit(solution)/shard_map/ppermute | solution.py:12
  4.6 2.9 %collective-permute-done = bf16[1,4,2,96,128]{4,3,2,1,0:T(8,128)(2,1)S(1)} collective-permute-done((bf16[1,4,2,96,128]{4,3,2,1,0:T(8,128)(2,1)}, bf16[1,4,2,96,128]{4,3,2,1,0:T(8,128)(2,1)S(1)}, u32[]{:S(2)}, u32[]{:S(2)}) %collective-permute-start) | collective-permute-done | bytes 196640 | tf_op jit(solution)/shard_map/ppermute | solution.py:12
  7.6 1.0 %constant_dynamic-update-slice_fusion = bf16[1,8,2,96,128]{4,3,2,1,0:T(8,128)(2,1)S(1)} fusion(bf16[1,8,2,96,128]{4,3,2,1,0:T(8,128)(2,1)S(1)} %constant_dynamic-update-slice_fusion.1, bf16[1,4,2,96,128]{4,3,2,1,0:T(8,128)(2,1)} %param.7), kind=kLoop, calls=%fused_computation.216 | loop fusion | bytes 393216 | tf_op jit(solution)/shard_map/concatenate | solution.py:64
  8.5 3.2 %collective-permute-start.1 = (bf16[1,8,2,96,128]{4,3,2,1,0:T(8,128)(2,1)S(1)}, bf16[1,8,2,96,128]{4,3,2,1,0:T(8,128)(2,1)S(1)}, u32[]{:S(2)}, u32[]{:S(2)}) collective-permute-start(bf16[1,8,2,96,128]{4,3,2,1,0:T(8,128)(2,1)S(1)} %constant_dynamic-update-slice_fusion), channel_id=1, source_target_pairs={{0,4},{4,8},{8,12},{1,5},{5,9},{9,13},{2,6},{6,10},{10,14},{3,7},{... | collective-permute-start | bytes 1179656 | tf_op jit(solution)/shard_map/ppermute | solution.py:23
  11.7 1.3 %collective-permute-start.2 = (bf16[1,8,2,96,128]{4,3,2,1,0:T(8,128)(2,1)S(1)}, bf16[1,8,2,96,128]{4,3,2,1,0:T(8,128)(2,1)S(1)}, u32[]{:S(2)}, u32[]{:S(2)}) collective-permute-start(bf16[1,8,2,96,128]{4,3,2,1,0:T(8,128)(2,1)S(1)} %constant_dynamic-update-slice_fusion), channel_id=1, source_target_pairs={{4,0},{8,4},{12,8},{5,1},{9,5},{13,9},{6,2},{10,6},{14,10},{7,3},{... | collective-permute-start | bytes 1179656 | tf_op jit(solution)/shard_map/ppermute | solution.py:25
  13.2 5.0 %collective-permute-done.1 = bf16[1,8,2,96,128]{4,3,2,1,0:T(8,128)(2,1)S(1)} collective-permute-done((bf16[1,8,2,96,128]{4,3,2,1,0:T(8,128)(2,1)S(1)}, bf16[1,8,2,96,128]{4,3,2,1,0:T(8,128)(2,1)S(1)}, u32[]{:S(2)}, u32[]{:S(2)}) %collective-permute-start.1) | collective-permute-done | bytes 393248 | tf_op jit(solution)/shard_map/ppermute | solution.py:23
  18.2 4.1 %collective-permute-done.2 = bf16[1,8,2,96,128]{4,3,2,1,0:T(8,128)(2,1)S(1)} collective-permute-done((bf16[1,8,2,96,128]{4,3,2,1,0:T(8,128)(2,1)S(1)}, bf16[1,8,2,96,128]{4,3,2,1,0:T(8,128)(2,1)S(1)}, u32[]{:S(2)}, u32[]{:S(2)}) %collective-permute-start.2) | collective-permute-done | bytes 393248 | tf_op jit(solution)/shard_map/ppermute | solution.py:25
  22.6 0.8 %fusion.7 = bf16[1,8,6,96,128]{4,3,2,1,0:T(8,128)(2,1)S(1)} fusion(f32[96]{0:T(128)S(1)} %copy-done.2, f32[8,6,128]{2,1,0:T(8,128)S(1)} %add_rsqrt_fusion, bf16[1,8,2,96,128]{4,3,2,1,0:T(8,128)(2,1)S(1)} %collective-permute-done.2, bf16[1,8,2,96,128]{4,3,2,1,0:T(8,128)(2,1)S(1)} %constant_dynamic-update-slice_fusion, ...), kind=kLoop, calls=%fused_computation.45 | loop fusion | flops 5898240 | bytes 2384256 | tf_op jit(solution)/shard_map/convert_element_type | solution.py:66
  23.4 3.0 %pad_slice_fusion.1 = (bf16[1,6,4,96,128]{4,3,2,1,0:T(8,128)(2,1)S(1)}, bf16[1,6,4,96,128]{4,3,2,1,0:T(8,128)(2,1)S(1)}, bf16[1,6,4,96,128]{4,3,2,1,0:T(8,128)(2...) fusion(bf16[1,8,6,96,128]{4,3,2,1,0:T(8,128)(2,1)S(1)} %fusion.7), kind=kLoop, calls=%fused_computation.1 | loop fusion | bytes 13565952 | tf_op jit(solution)/shard_map/slice | solution.py:49
  26.4 0.8 %fusion.164 = (bf16[1,6,4,96,128]{4,3,2,1,0:T(8,128)(2,1)S(1)}, bf16[1,6,4,96,128]{4,3,2,1,0:T(8,128)(2,1)S(1)}, bf16[1,6,4,96,128]{4,3,2,1,0:T(8,128)(2,1)S(1)}...) fusion(bf16[1,8,6,96,128]{4,3,2,1,0:T(8,128)(2,1)S(1)} %fusion.7), kind=kLoop, calls=%fused_computation.239 | loop fusion | bytes 10027008 | tf_op jit(solution)/shard_map/slice | solution.py:49
  27.4 0.6 %fusion.13 = f32[6,4,128,96]{2,3,1,0:T(8,128)S(1)} fusion(bf16[1,6,4,96,128]{4,3,2,1,0:T(8,128)(2,1)S(1)} %get-tuple-element.8, bf16[1,6,4,96,128]{4,3,2,1,0:T(8,128)(2,1)S(1)} %get-tuple-element.29, bf16[1,6,4,96,128]{4,3,2,1,0:T(8,128)(2,1)S(1)} %get-tuple-element.7, bf16[96,2592]{1,0:T(8,128)(2,1)S(1)} %copy-done.3), kind=kOutput, calls=%fused_computation.53 | convolution fusion | flops 175177728 | bytes 3022848 | tf_op jit(solution)/shard_map/oc,bfrcw->bfrow/dot_general | solution.py:54
  28.1 0.6 %fusion.61 = f32[6,4,128,96]{2,3,1,0:T(8,128)S(1)} fusion(f32[6,4,128,96]{2,3,1,0:T(8,128)S(1)} %fusion.13, bf16[1,6,4,96,128]{4,3,2,1,0:T(8,128)(2,1)S(1)} %get-tuple-element.6, bf16[1,6,4,96,128]{4,3,2,1,0:T(8,128)(2,1)S(1)} %get-tuple-element.30, bf16[1,6,4,96,128]{4,3,2,1,0:T(8,128)(2,1)S(1)} %get-tuple-element.31, bf16[96,2592]{1,0:T(8,128)(2,1)S(1)} %copy-done.3), kind=kOutput, calls=%fused_computation.108 | convolution fusion | flops 175472640 | bytes 4202496 | tf_op jit(solution)/shard_map/oc,bfrcw->bfrow/dot_general | solution.py:54
  28.6 0.6 %fusion.60 = f32[6,4,128,96]{2,3,1,0:T(8,128)S(1)} fusion(f32[6,4,128,96]{2,3,1,0:T(8,128)S(1)} %fusion.61, bf16[1,6,4,96,128]{4,3,2,1,0:T(8,128)(2,1)S(1)} %get-tuple-element.10, bf16[1,6,4,96,128]{4,3,2,1,0:T(8,128)(2,1)S(1)} %get-tuple-element.28, bf16[1,6,4,96,128]{4,3,2,1,0:T(8,128)(2,1)S(1)} %get-tuple-element.9, bf16[96,2592]{1,0:T(8,128)(2,1)S(1)} %copy-done.3), kind=kOutput, calls=%fused_computation.107 | convolution fusion | flops 175472640 | bytes 4202496 | tf_op jit(solution)/shard_map/oc,bfrcw->bfrow/dot_general | solution.py:54
  29.3 0.6 %fusion.59 = f32[6,4,128,96]{2,3,1,0:T(8,128)S(1)} fusion(f32[6,4,128,96]{2,3,1,0:T(8,128)S(1)} %fusion.60, bf16[1,6,4,96,128]{4,3,2,1,0:T(8,128)(2,1)S(1)} %get-tuple-element.12, bf16[1,6,4,96,128]{4,3,2,1,0:T(8,128)(2,1)S(1)} %get-tuple-element.27, bf16[1,6,4,96,128]{4,3,2,1,0:T(8,128)(2,1)S(1)} %get-tuple-element.11, bf16[96,2592]{1,0:T(8,128)(2,1)S(1)} %copy-done.3), kind=kOutput, calls=%fused_computation.106 | convolution fusion | flops 175472640 | bytes 4202496 | tf_op jit(solution)/shard_map/oc,bfrcw->bfrow/dot_general | solution.py:54
  29.9 0.6 %fusion.58 = f32[6,4,128,96]{2,3,1,0:T(8,128)S(1)} fusion(f32[6,4,128,96]{2,3,1,0:T(8,128)S(1)} %fusion.59, bf16[1,6,4,96,128]{4,3,2,1,0:T(8,128)(2,1)S(1)} %get-tuple-element.14, bf16[1,6,4,96,128]{4,3,2,1,0:T(8,128)(2,1)S(1)} %get-tuple-element.26, bf16[1,6,4,96,128]{4,3,2,1,0:T(8,128)(2,1)S(1)} %get-tuple-element.13, bf16[96,2592]{1,0:T(8,128)(2,1)S(1)} %copy-done.3), kind=kOutput, calls=%fused_computation.105 | convolution fusion | flops 175472640 | bytes 4202496 | tf_op jit(solution)/shard_map/oc,bfrcw->bfrow/dot_general | solution.py:54
  30.5 0.6 %fusion.57 = f32[6,4,128,96]{2,3,1,0:T(8,128)S(1)} fusion(f32[6,4,128,96]{2,3,1,0:T(8,128)S(1)} %fusion.58, bf16[1,6,4,96,128]{4,3,2,1,0:T(8,128)(2,1)S(1)} %get-tuple-element.16, bf16[1,6,4,96,128]{4,3,2,1,0:T(8,128)(2,1)S(1)} %get-tuple-element.25, bf16[1,6,4,96,128]{4,3,2,1,0:T(8,128)(2,1)S(1)} %get-tuple-element.15, bf16[96,2592]{1,0:T(8,128)(2,1)S(1)} %copy-done.3), kind=kOutput, calls=%fused_computation.104 | convolution fusion | flops 175472640 | bytes 4202496 | tf_op jit(solution)/shard_map/oc,bfrcw->bfrow/dot_general | solution.py:54
  31.1 0.6 %fusion.56 = f32[6,4,128,96]{2,3,1,0:T(8,128)S(1)} fusion(f32[6,4,128,96]{2,3,1,0:T(8,128)S(1)} %fusion.57, bf16[1,6,4,96,128]{4,3,2,1,0:T(8,128)(2,1)S(1)} %get-tuple-element.18, bf16[1,6,4,96,128]{4,3,2,1,0:T(8,128)(2,1)S(1)} %get-tuple-element.24, bf16[1,6,4,96,128]{4,3,2,1,0:T(8,128)(2,1)S(1)} %get-tuple-element.17, bf16[96,2592]{1,0:T(8,128)(2,1)S(1)} %copy-done.3), kind=kOutput, calls=%fused_computation.103 | convolution fusion | flops 175472640 | bytes 4202496 | tf_op jit(solution)/shard_map/oc,bfrcw->bfrow/dot_general | solution.py:54
  31.7 0.6 %fusion.55 = f32[6,4,128,96]{2,3,1,0:T(8,128)S(1)} fusion(f32[6,4,128,96]{2,3,1,0:T(8,128)S(1)} %fusion.56, bf16[1,6,4,96,128]{4,3,2,1,0:T(8,128)(2,1)S(1)} %get-tuple-element.20, bf16[1,6,4,96,128]{4,3,2,1,0:T(8,128)(2,1)S(1)} %get-tuple-element.23, bf16[1,6,4,96,128]{4,3,2,1,0:T(8,128)(2,1)S(1)} %get-tuple-element.19, bf16[96,2592]{1,0:T(8,128)(2,1)S(1)} %copy-done.3), kind=kOutput, calls=%fused_computation.102 | convolution fusion | flops 175472640 | bytes 4202496 | tf_op jit(solution)/shard_map/oc,bfrcw->bfrow/dot_general | solution.py:54
  32.4 0.6 %multiply_reduce_fusion = (f32[6,4,128]{2,1,0:T(4,128)S(1)}, f32[1,6,4,128,96]{3,4,2,1,0:T(8,128)S(1)}) fusion(f32[96]{0:T(128)S(1)} %copy-done.5, f32[6,4,128,96]{2,3,1,0:T(8,128)S(1)} %fusion.55, bf16[1,6,4,96,128]{4,3,2,1,0:T(8,128)(2,1)S(1)} %get-tuple-element.21, bf16[1,6,4,96,128]{4,3,2,1,0:T(8,128)(2,1)S(1)} %get-tuple-element.22, ...), kind=kOutput, calls=%fused_computation.128 | convolution fusion | flops 176354304 | bytes 4215296 | tf_op jit(solution)/shard_map/oc,bfrcw->bfrow/dot_general | solution.py:54
  33.0 0.4 %fusion.109 = bf16[1,6,4,96,128]{4,3,2,1,0:T(8,128)(2,1)S(1)} fusion(f32[96]{0:T(128)S(1)} %copy-done.1, f32[1,6,4,128,96]{3,4,2,1,0:T(8,128)S(1)} %get-tuple-element.60, f32[6,4,128]{2,1,0:T(4,128)S(1)} %add_rsqrt_fusion.1, pred[6,4]{1,0:T(8,128)(4,1)S(1)} %broadcast_and_fusion), kind=kLoop, calls=%fused_computation.177 | loop fusion | flops 2359296 | bytes 1782168 | tf_op jit(solution)/shard_map/jit(_where)/select_n | solution.py:73
  33.5 1.0 %pad_slice_fusion.19 = (bf16[1,4,2,96,128]{4,3,2,1,0:T(8,128)(2,1)S(1)}, bf16[1,4,2,96,128]{4,3,2,1,0:T(8,128)(2,1)S(1)}, bf16[1,4,2,96,128]{4,3,2,1,0:T(8,128)(...) fusion(bf16[1,6,4,96,128]{4,3,2,1,0:T(8,128)(2,1)S(1)} %fusion.109), kind=kLoop, calls=%fused_computation.19 | loop fusion | bytes 4718592 | tf_op jit(solution)/shard_map/slice | solution.py:49
  34.5 0.3 fusion.165
  34.8 0.7 %copy-done.4 = bf16[96,2592]{1,0:T(8,128)(2,1)S(1)} copy-done((bf16[96,2592]{1,0:T(8,128)(2,1)S(1)}, bf16[96,2592]{1,0:T(8,128)(2,1)}, u32[]{:S(2)}) %copy-start.4) | copy-done | bytes 497688
  35.8 0.3 convolution_add_fusion.7
  36.1 0.3 convolution_add_fusion.6
  36.4 0.3 convolution_add_fusion.5
  36.8 0.3 convolution_add_fusion.4
  37.1 0.3 convolution_add_fusion.3
  37.4 0.3 convolution_add_fusion.2
  37.7 0.3 convolution_add_fusion.1
  38.1 0.6 %copy-done = bf16[1,4,2,96,128]{4,3,2,1,0:T(8,128)(2,1)S(1)} copy-done((bf16[1,4,2,96,128]{4,3,2,1,0:T(8,128)(2,1)S(1)}, bf16[1,4,2,96,128]{4,3,2,1,0:T(8,128)(2,1)}, u32[]{:S(2)}) %copy-start) | copy-done | bytes 196632
  38.7 1.0 %fusion.71 = bf16[1,4,2,96,128]{4,3,2,1,0:T(8,128)(2,1)} fusion(f32[4,2,128,96]{2,3,1,0:T(8,128)S(1)} %convolution_add_fusion.1, bf16[1,4,2,96,128]{4,3,2,1,0:T(8,128)(2,1)S(1)} %get-tuple-element.48, bf16[1,4,2,96,128]{4,3,2,1,0:T(8,128)(2,1)S(1)} %get-tuple-element.49, bf16[1,4,2,96,128]{4,3,2,1,0:T(8,128)(2,1)S(1)} %get-tuple-element.32, ...), kind=kOutput, calls=%fused_computation.130 | convolution fusion | flops 58884096 | bytes 1450496 | tf_op jit(solution)/shard_map/oc,bfrcw->bfrow/dot_general | solution.py:54
  (20 shorter events, 1.0 us)
Async XLA Ops:
  0.0 22.6 %copy-start.2 = (f32[96]{0:T(128)S(1)}, f32[96]{0:T(128)}, u32[]{:S(2)}) copy-start(f32[96]{0:T(128)} %param.8) | copy-start | bytes 1156
  0.0 7.5 %collective-permute-start = (bf16[1,4,2,96,128]{4,3,2,1,0:T(8,128)(2,1)}, bf16[1,4,2,96,128]{4,3,2,1,0:T(8,128)(2,1)S(1)}, u32[]{:S(2)}, u32[]{:S(2)}) collective-permute-start(bf16[1,4,2,96,128]{4,3,2,1,0:T(8,128)(2,1)} %param.7), channel_id=1, source_target_pairs={{0,1},{1,2},{2,3},{4,5},{5,6},{6,7},{8,9},{9,10},{10,11},{12,13},{... | collective-permute-start | bytes 589832 | tf_op jit(solution)/shard_map/ppermute | solution.py:12
  8.5 9.7 %collective-permute-start.1 = (bf16[1,8,2,96,128]{4,3,2,1,0:T(8,128)(2,1)S(1)}, bf16[1,8,2,96,128]{4,3,2,1,0:T(8,128)(2,1)S(1)}, u32[]{:S(2)}, u32[]{:S(2)}) collective-permute-start(bf16[1,8,2,96,128]{4,3,2,1,0:T(8,128)(2,1)S(1)} %constant_dynamic-update-slice_fusion), channel_id=1, source_target_pairs={{0,4},{4,8},{8,12},{1,5},{5,9},{9,13},{2,6},{6,10},{10,14},{3,7},{... | collective-permute-start | bytes 1179656 | tf_op jit(solution)/shard_map/ppermute | solution.py:23
  11.7 10.6 %collective-permute-start.2 = (bf16[1,8,2,96,128]{4,3,2,1,0:T(8,128)(2,1)S(1)}, bf16[1,8,2,96,128]{4,3,2,1,0:T(8,128)(2,1)S(1)}, u32[]{:S(2)}, u32[]{:S(2)}) collective-permute-start(bf16[1,8,2,96,128]{4,3,2,1,0:T(8,128)(2,1)S(1)} %constant_dynamic-update-slice_fusion), channel_id=1, source_target_pairs={{4,0},{8,4},{12,8},{5,1},{9,5},{13,9},{6,2},{10,6},{14,10},{7,3},{... | collective-permute-start | bytes 1179656 | tf_op jit(solution)/shard_map/ppermute | solution.py:25
  26.4 1.0 %copy-start.3 = (bf16[96,2592]{1,0:T(8,128)(2,1)S(1)}, bf16[96,2592]{1,0:T(8,128)(2,1)}, u32[]{:S(2)}) copy-start(bf16[96,2592]{1,0:T(8,128)(2,1)} %param.9) | copy-start | bytes 1492996
  31.7 0.7 %copy-start.5 = (f32[96]{0:T(128)S(1)}, f32[96]{0:T(128)}, u32[]{:S(2)}) copy-start(f32[96]{0:T(128)} %param.10) | copy-start | bytes 1156
  32.4 0.7 %copy-start.1 = (f32[96]{0:T(128)S(1)}, f32[96]{0:T(128)}, u32[]{:S(2)}) copy-start(f32[96]{0:T(128)} %param.11) | copy-start | bytes 1156
  34.5 1.0 %copy-start.4 = (bf16[96,2592]{1,0:T(8,128)(2,1)S(1)}, bf16[96,2592]{1,0:T(8,128)(2,1)}, u32[]{:S(2)}) copy-start(bf16[96,2592]{1,0:T(8,128)(2,1)} %param.12) | copy-start | bytes 1492996
  37.7 0.9 %copy-start = (bf16[1,4,2,96,128]{4,3,2,1,0:T(8,128)(2,1)S(1)}, bf16[1,4,2,96,128]{4,3,2,1,0:T(8,128)(2,1)}, u32[]{:S(2)}) copy-start(bf16[1,4,2,96,128]{4,3,2,1,0:T(8,128)(2,1)} %param.7) | copy-start | bytes 589828
  37.7 0.9 %copy-start.6 = (f32[96]{0:T(128)S(1)}, f32[96]{0:T(128)}, u32[]{:S(2)}) copy-start(f32[96]{0:T(128)} %param.13) | copy-start | bytes 1156
where the time goes:
time: 39.9 us; the launch traced here: 39.6 us
  waiting for transfers between devices  12.1 us (30%)
  starting transfers between devices  9.14 us (23%)
  matrix products  8.97 us (22%)
  local copies, waits for them, and re-layouts  7.62 us (19%)
  other arithmetic  1.58 us (4%)
    dot_general x18, matrix products, conv_valid(): jnp.einsum('oc,bfrcw->bfrow', columns, stacked, preferred_element_type=jn...  8.97 us
    ppermute x1, waiting for transfers between devices, padded_2(): lax.ppermute(tail, axis, [(i, (i + 1) % count) for i in range(ends)])  5.04 us
    ppermute x1, starting transfers between devices, passed_along(): return lax.ppermute(block, axis, route)  4.62 us
    ppermute x1, waiting for transfers between devices, padded_2(): lax.ppermute(head, axis, [((i + 1) % count, i) for i in range(ends)])  4.12 us
    slice x2, local copies, waits for them, and re-layouts, conv_valid(): section[..., 0:width]  3.97 us
    ppermute x1, starting transfers between devices, padded_2(): lax.ppermute(tail, axis, [(i, (i + 1) % count) for i in range(ends)])  3.22 us
    ppermute x1, waiting for transfers between devices, passed_along(): return lax.ppermute(block, axis, route)  2.9 us
    unnamed x15, local copies, waits for them, and re-layouts  1.61 us
  transfers between devices with their start and end apart: 3, of which 3 were waited for; matrix products, arithmetic and copies ran while one was open for 0% of the time, Pallas kernels for 0%

commit v1 on v0

v1 whole, which is shorter than its diff:
```python
import jax
import jax.numpy as jnp
from jax import lax
from jax.experimental import pallas as pl
from jax.experimental.pallas import tpu as pltpu
from jax.sharding import PartitionSpec as P

MESH = pl.DeviceIdType.MESH
epsilon = 1e-06


def block_kernel(
    video, k_first, k_second, g_first, b_first, g_second, b_second, out,
    ext_a, ext_b, st_a, st_b, w_a, w_b, vecs, local_sem, send_sem, recv_sem,
):
    frames, rows, chans, width = video.shape[1:]
    group = 9 * chans
    t = lax.axis_index("tm")
    r = lax.axis_index("rows")
    has_prev = t > 0
    has_next = t < lax.axis_size("tm") - 1
    has_up = r > 0
    has_down = r < lax.axis_size("rows") - 1

    def both(one, other):
        return jnp.logical_and(one, other)

    up, down = {"rows": r - 1}, {"rows": r + 1}
    later = {"tm": t + 1}
    later_up, later_down = {"tm": t + 1, "rows": r - 1}, {"tm": t + 1, "rows": r + 1}

    own = pltpu.make_async_copy(video.at[0], ext_a.at[2:, 1 : rows + 1], local_sem.at[0])
    load_a = pltpu.make_async_copy(k_first, w_a, local_sem.at[1])
    load_b = pltpu.make_async_copy(k_second, w_b, local_sem.at[2])
    own.start()
    load_a.start()
    load_b.start()

    barrier = pltpu.get_barrier_semaphore()
    prev, prev_up, prev_down = {"tm": t - 1}, {"tm": t - 1, "rows": r - 1}, {"tm": t - 1, "rows": r + 1}
    for cond, where in (
        (has_up, up), (has_down, down), (has_prev, prev),
        (both(has_prev, has_up), prev_up), (both(has_prev, has_down), prev_down),
    ):
        @pl.when(cond)
        def _():
            pl.semaphore_signal(barrier, inc=1, device_id=where, device_id_type=MESH)
    beside = has_up.astype(jnp.int32) + has_down.astype(jnp.int32)
    pl.semaphore_wait(barrier, beside + has_next.astype(jnp.int32) * (1 + beside))

    def copies(source, ext, first, last, slot, over_time):
        f = slice(first, last)
        e = slice(first + 2, last + 2)
        plan = [
            (source.at[f, 0], ext.at[e, rows + 1], up, has_up, has_down),
            (source.at[f, rows - 1], ext.at[e, 0], down, has_down, has_up),
        ]
        if over_time:
            h = slice(frames - 2, frames)
            z = slice(0, 2)
            plan += [
                (source.at[h, 0:rows], ext.at[z, 1 : rows + 1], later, has_next, has_prev),
                (source.at[h, 0], ext.at[z, rows + 1], later_up, both(has_next, has_up), both(has_prev, has_down)),
                (source.at[h, rows - 1], ext.at[z, 0], later_down, both(has_next, has_down), both(has_prev, has_up)),
            ]
        made = []
        for n, (src, dst, where, sends, takes) in enumerate(plan):
            copy = pltpu.make_async_remote_copy(
                src_ref=src, dst_ref=dst, send_sem=send_sem.at[slot + n], recv_sem=recv_sem.at[slot + n],
                device_id=where, device_id_type=MESH,
            )
            made.append((copy, sends, takes))
        return made

    def start(made):
        for copy, sends, _ in made:
            pl.when(sends)(copy.start)

    def taken(made):
        for copy, _, takes in made:
            pl.when(takes)(copy.wait_recv)

    def sent(made):
        for copy, sends, _ in made:
            pl.when(sends)(copy.wait_send)

    moved = copies(video.at[0], ext_a, 0, frames, 0, True)
    start(moved)

    for ext in (ext_a, ext_b):
        @pl.when(jnp.logical_not(has_up))
        def _():
            ext[:, 0] = jnp.zeros((frames + 2, chans, width), jnp.bfloat16)

        @pl.when(jnp.logical_not(has_down))
        def _():
            ext[:, rows + 1] = jnp.zeros((frames + 2, chans, width), jnp.bfloat16)

        @pl.when(jnp.logical_not(has_prev))
        def _():
            ext[0:2] = jnp.zeros((2, rows + 2, chans, width), jnp.bfloat16)

    for n, ref in enumerate((g_first, b_first, g_second, b_second)):
        vecs[n] = jnp.broadcast_to(ref[...], (width, chans)).T

    lane = lax.broadcasted_iota(jnp.int32, (chans, width), 1)

    def act(values, gain):
        meansq = jnp.sum(values * values, axis=0, keepdims=True) * (1.0 / chans)
        half = values * lax.rsqrt(meansq + epsilon) * (gain * 0.5)
        return half + half * jnp.tanh(half)

    def place(stack, f, p, field):
        shifted = [
            jnp.where(lane == 0, 0.0, pltpu.roll(field, 1, 1)).astype(jnp.bfloat16),
            field.astype(jnp.bfloat16),
            jnp.where(lane == width - 1, 0.0, pltpu.roll(field, width - 1, 1)).astype(jnp.bfloat16),
        ]
        for row in range(rows):
            j = p - row
            if 0 <= j < 3:
                for k in range(3):
                    at = f * group + (j * 3 + k) * chans
                    stack[at : at + chans, row * width : (row + 1) * width] = shifted[k]

    def first_at(f, p):
        place(st_a, f, p, act(ext_a[f, p].astype(jnp.float32), vecs[0]))

    def conv(weights, stack, f):
        return jnp.dot(
            weights[...], stack[f * group : (f + 3) * group, :], preferred_element_type=jnp.float32
        )

    def second_of(f):
        total = conv(w_a, st_a, f)
        for row in range(rows):
            value = act(total[:, row * width : (row + 1) * width] + vecs[1], vecs[2])
            ext_b[f + 2, row + 1] = value.astype(jnp.bfloat16)
            place(st_b, f + 2, row + 1, value)

    def encoded_of(f):
        total = conv(w_b, st_b, f)
        for row in range(rows):
            value = total[:, row * width : (row + 1) * width] + vecs[3]
            out[0, f, row] = (ext_a[f + 2, row + 1].astype(jnp.float32) + value).astype(jnp.bfloat16)

    own.wait()
    for f in range(2, frames + 2):
        for p in range(1, rows + 1):
            first_at(f, p)
    load_a.wait()
    taken(moved[:2])
    for f in range(2, frames + 2):
        for p in (0, rows + 1):
            first_at(f, p)
    for f in range(2, frames):
        second_of(f)
    send_late = copies(ext_b.at[2:, 1 : rows + 1], ext_b, 2, frames, 5, True)
    start(send_late)
    taken(moved[2:])
    for f in range(2):
        for p in range(rows + 2):
            first_at(f, p)
    for f in range(2):
        second_of(f)
    send_early = copies(ext_b.at[2:, 1 : rows + 1], ext_b, 0, 2, 10, False)
    start(send_early)
    load_b.wait()
    taken(send_late)
    for f in range(2):
        for p in range(rows + 2):
            place(st_b, f, p, ext_b[f, p].astype(jnp.float32))
    for f in range(4, frames + 2):
        for p in (0, rows + 1):
            place(st_b, f, p, ext_b[f, p].astype(jnp.float32))
    taken(send_early)
    for f in range(2, 4):
        for p in (0, rows + 1):
            place(st_b, f, p, ext_b[f, p].astype(jnp.float32))
    for f in range(frames):
        encoded_of(f)
    sent(moved)
    sent(send_late)
    sent(send_early)


def local(video, gamma_first, kernel_first, bias_first, gamma_second, kernel_second, bias_second):
    frames, rows, chans, width = video.shape[1:]
    ext = pltpu.VMEM((frames + 2, rows + 2, chans, width), jnp.bfloat16)
    stack = pltpu.VMEM(((frames + 2) * 9 * chans, rows * width), jnp.bfloat16)
    weights = pltpu.VMEM(kernel_first.shape, jnp.bfloat16)
    vmem = pl.BlockSpec(memory_space=pltpu.VMEM)
    hbm = pl.BlockSpec(memory_space=pl.ANY)
    return pl.pallas_call(
        block_kernel,
        out_shape=jax.ShapeDtypeStruct(video.shape, jnp.bfloat16),
        in_specs=[hbm] * 3 + [vmem] * 4,
        out_specs=vmem,
        scratch_shapes=[
            ext, ext, stack, stack, weights, weights,
            pltpu.VMEM((4, chans, width), jnp.float32),
            pltpu.SemaphoreType.DMA((3,)),
            pltpu.SemaphoreType.DMA((12,)),
            pltpu.SemaphoreType.DMA((12,)),
        ],
        compiler_params=pltpu.CompilerParams(collective_id=0, has_side_effects=True),
        name="residual_block",
    )(
        video, kernel_first, kernel_second, gamma_first[None, :], bias_first[None, :],
        gamma_second[None, :], bias_second[None, :],
    )


def solution(mesh):
    in_specs = (P("groups", "tm", "rows", None, None), P(), P(), P(), P(), P(), P())
    out_specs = P("groups", "tm", "rows", None, None)
    return jax.shard_map(local, mesh=mesh, in_specs=in_specs, out_specs=out_specs, check_vma=False)
```

time: 39.9 us -> 19.5 us (0.49)
  the two profiles are of different devices: /device:TPU:1 before, /device:TPU:0 now
where the time goes in v1:
time: 19.5 us; the launch traced here: 19.4 us
  Pallas kernels  17.8 us (91%)
  local copies, waits for them, and re-layouts  1.62 us (8%)
    pallas_call x1, Pallas kernels, local(): pl.pallas_call(block_kernel, out_shape=jax.ShapeDtypeStruct(video.shape,...  17.8 us
    unnamed x1, local copies, waits for them, and re-layouts  1.62 us

profile of v1, /device:TPU:0, one launch (start us, length us, event | category | flops | bytes accessed | tf_op | source)
XLA Modules:
  0.0 19.4 jit_solution(14279159914605399631)
XLA Ops:
  0.0 17.8 %residual_block.1 = bf16[1,4,2,96,128]{4,3,2,1,0:T(8,128)(2,1)} custom-call(bf16[1,4,2,96,128]{4,3,2,1,0:T(8,128)(2,1)} %video.1, bf16[96,2592]{1,0:T(8,128)(2,1)} %k_first.1, bf16[96,2592]{1,0:T(8,128)(2,1)} %k_second.1, f32[1,96]{1,0:T(1,128)} %bitcast.4, f32[1,96]{1,0:T(1,128)} %bitcast.5, f32[1,96]{1,0:T(1,128)} %bitcast.6, f32[1,96]{1,0:T(1,128)} %bitcast.7), custom_call_target="tpu_custom_call" | custom-call | tf_op jit(solution)/shard_map/residual_block/pallas_call | solution.py:194
  17.8 1.6 %copy.9 = bf16[1,4,2,96,128]{4,3,2,1,0:T(8,128)(2,1)} copy(bf16[1,4,2,96,128]{4,3,2,1,0:T(8,128)(2,1)} %residual_block.1) | data formatting | bytes 393216

commit v2 on v1

--- a/solution.py
+++ b/solution.py
@@ -11,7 +11,7 @@
 
 def block_kernel(
     video, k_first, k_second, g_first, b_first, g_second, b_second, out,
-    ext_a, ext_b, st_a, st_b, w_a, w_b, vecs, local_sem, send_sem, recv_sem,
+    ext_a, ext_b, st_a, st_b, w_a, w_b, vecs, small_0, small_1, small_2, small_3, local_sem, send_sem, recv_sem,
 ):
     frames, rows, chans, width = video.shape[1:]
     group = 9 * chans
@@ -29,13 +29,6 @@
     later = {"tm": t + 1}
     later_up, later_down = {"tm": t + 1, "rows": r - 1}, {"tm": t + 1, "rows": r + 1}
 
-    own = pltpu.make_async_copy(video.at[0], ext_a.at[2:, 1 : rows + 1], local_sem.at[0])
-    load_a = pltpu.make_async_copy(k_first, w_a, local_sem.at[1])
-    load_b = pltpu.make_async_copy(k_second, w_b, local_sem.at[2])
-    own.start()
-    load_a.start()
-    load_b.start()
-
     barrier = pltpu.get_barrier_semaphore()
     prev, prev_up, prev_down = {"tm": t - 1}, {"tm": t - 1, "rows": r - 1}, {"tm": t - 1, "rows": r + 1}
     for cond, where in (
@@ -45,6 +38,22 @@
         @pl.when(cond)
         def _():
             pl.semaphore_signal(barrier, inc=1, device_id=where, device_id_type=MESH)
+    own = pltpu.make_async_copy(video.at[0], ext_a.at[2:, 1 : rows + 1], local_sem.at[0])
+    load_a = pltpu.make_async_copy(k_first, w_a, local_sem.at[1])
+    load_b = pltpu.make_async_copy(k_second, w_b, local_sem.at[2])
+    own.start()
+    small = [
+        pltpu.make_async_copy(src, dst, local_sem.at[3 + n])
+        for n, (src, dst) in enumerate(
+            ((g_first, small_0), (b_first, small_1), (g_second, small_2), (b_second, small_3))
+        )
+    ]
+    for copy in small:
+        copy.start()
+    load_a.start()
+    load_b.start()
+
+    own.wait()
     beside = has_up.astype(jnp.int32) + has_down.astype(jnp.int32)
     pl.semaphore_wait(barrier, beside + has_next.astype(jnp.int32) * (1 + beside))
 
@@ -84,7 +93,7 @@
         for copy, sends, _ in made:
             pl.when(sends)(copy.wait_send)
 
-    moved = copies(video.at[0], ext_a, 0, frames, 0, True)
+    moved = copies(ext_a.at[2:, 1 : rows + 1], ext_a, 0, frames, 0, True)
     start(moved)
 
     for ext in (ext_a, ext_b):
@@ -100,7 +109,8 @@
         def _():
             ext[0:2] = jnp.zeros((2, rows + 2, chans, width), jnp.bfloat16)
 
-    for n, ref in enumerate((g_first, b_first, g_second, b_second)):
+    for n, ref in enumerate((small_0, small_1, small_2, small_3)):
+        small[n].wait()
         vecs[n] = jnp.broadcast_to(ref[...], (width, chans)).T
 
     lane = lax.broadcasted_iota(jnp.int32, (chans, width), 1)
@@ -144,7 +154,6 @@
             value = total[:, row * width : (row + 1) * width] + vecs[3]
             out[0, f, row] = (ext_a[f + 2, row + 1].astype(jnp.float32) + value).astype(jnp.bfloat16)
 
-    own.wait()
     for f in range(2, frames + 2):
         for p in range(1, rows + 1):
             first_at(f, p)
@@ -193,13 +202,14 @@
     hbm = pl.BlockSpec(memory_space=pl.ANY)
     return pl.pallas_call(
         block_kernel,
-        out_shape=jax.ShapeDtypeStruct(video.shape, jnp.bfloat16),
-        in_specs=[hbm] * 3 + [vmem] * 4,
+        out_shape=pltpu.VMEM(video.shape, jnp.bfloat16),
+        in_specs=[hbm] * 7,
         out_specs=vmem,
         scratch_shapes=[
             ext, ext, stack, stack, weights, weights,
             pltpu.VMEM((4, chans, width), jnp.float32),
-            pltpu.SemaphoreType.DMA((3,)),
+            *[pltpu.VMEM((1, chans), jnp.float32)] * 4,
+            pltpu.SemaphoreType.DMA((7,)),
             pltpu.SemaphoreType.DMA((12,)),
             pltpu.SemaphoreType.DMA((12,)),
         ],

time: 19.5 us -> 17 us (0.87)
  Pallas kernels: 17.8 us -> 16.2 us
  local copies, waits for them, and re-layouts: 1.62 us -> 0.68 us
    pallas_call x1, Pallas kernels: 17.8 us -> 16.2 us  [local(): pl.pallas_call(block_kernel, out_shape=pltpu.VMEM(video.shape, jnp.bfloat...]
    unnamed x1, local copies, waits for them, and re-layouts: 1.62 us -> 0.68 us
where the time goes in v2:
time: 17 us; the launch traced here: 16.9 us
  Pallas kernels  16.2 us (95%)
  local copies, waits for them, and re-layouts  0.68 us (4%)
    pallas_call x1, Pallas kernels, local(): pl.pallas_call(block_kernel, out_shape=pltpu.VMEM(video.shape, jnp.bfloat...  16.2 us
    unnamed x1, local copies, waits for them, and re-layouts  0.68 us

profile of v2, /device:TPU:0, one launch (start us, length us, event | category | flops | bytes accessed | tf_op | source)
XLA Modules:
  0.0 16.9 jit_solution(1184976535102515437)
XLA Ops:
  0.0 16.2 %residual_block.1 = bf16[1,4,2,96,128]{4,3,2,1,0:T(8,128)(2,1)S(1)} custom-call(bf16[1,4,2,96,128]{4,3,2,1,0:T(8,128)(2,1)} %video.1, bf16[96,2592]{1,0:T(8,128)(2,1)} %k_first.1, bf16[96,2592]{1,0:T(8,128)(2,1)} %k_second.1, f32[1,96]{1,0:T(1,128)} %bitcast.4, f32[1,96]{1,0:T(1,128)} %bitcast.5, f32[1,96]{1,0:T(1,128)} %bitcast.6, f32[1,96]{1,0:T(1,128)} %bitcast.7), custom_call_target="tpu_custom_call" | custom-call | tf_op jit(solution)/shard_map/residual_block/pallas_call | solution.py:203
  16.2 0.7 %copy.9 = bf16[1,4,2,96,128]{4,3,2,1,0:T(8,128)(2,1)} copy(bf16[1,4,2,96,128]{4,3,2,1,0:T(8,128)(2,1)S(1)} %residual_block.1) | data formatting | bytes 393216

commit v3 on v2

v3 whole, which is shorter than its diff:
```python
import jax
import jax.numpy as jnp
from jax import lax
from jax.experimental import pallas as pl
from jax.experimental.pallas import tpu as pltpu
from jax.sharding import PartitionSpec as P

MESH = pl.DeviceIdType.MESH
epsilon = 1e-06


def block_kernel(
    video, k_first, k_second, g_first, b_first, g_second, b_second, out,
    ext, st_a, st_b, w_a, w_b, by_a, by_b, sum_a, sum_b, vecs, small_0, small_1, small_2, small_3, local_sem, send_sem, recv_sem,
):
    frames, rows, chans, width = video.shape[1:]
    group = 9 * chans
    t = lax.axis_index("tm")
    r = lax.axis_index("rows")
    has_prev = t > 0
    has_next = t < lax.axis_size("tm") - 1
    has_up = r > 0
    has_down = r < lax.axis_size("rows") - 1

    def both(one, other):
        return jnp.logical_and(one, other)

    up, down, later = {"rows": r - 1}, {"rows": r + 1}, {"tm": t + 1}

    barrier = pltpu.get_barrier_semaphore()
    for cond, where in ((has_up, up), (has_down, down), (has_prev, {"tm": t - 1})):
        @pl.when(cond)
        def _():
            pl.semaphore_signal(barrier, inc=1, device_id=where, device_id_type=MESH)

    own_rows = slice(2, 2 + rows)
    above, below = slice(0, 2), slice(2 + rows, 4 + rows)
    own = pltpu.make_async_copy(video.at[0], ext.at[frames:, own_rows], local_sem.at[0])
    load_a = pltpu.make_async_copy(k_first, w_a, local_sem.at[1])
    load_b = pltpu.make_async_copy(k_second, w_b, local_sem.at[2])
    own.start()
    small = [
        pltpu.make_async_copy(src, dst, local_sem.at[3 + n])
        for n, (src, dst) in enumerate(
            ((g_first, small_0), (b_first, small_1), (g_second, small_2), (b_second, small_3))
        )
    ]
    for copy in small:
        copy.start()
    load_a.start()
    load_b.start()

    own.wait()
    pl.semaphore_wait(
        barrier, has_up.astype(jnp.int32) + has_down.astype(jnp.int32) + has_next.astype(jnp.int32)
    )

    order = list(range(frames))[::-1]

    def plan(slot, src, dst, where, sends, takes):
        copy = pltpu.make_async_remote_copy(
            src_ref=src, dst_ref=dst, send_sem=send_sem.at[slot], recv_sem=recv_sem.at[slot],
            device_id=where, device_id_type=MESH,
        )
        return copy, sends, takes

    beside, passed = {}, {}
    for f in range(frames):
        mine = ext.at[frames + f, own_rows]
        beside[f] = (
            plan(f, mine, ext.at[frames + f, below], up, has_up, has_down),
            plan(frames + f, mine, ext.at[frames + f, above], down, has_down, has_up),
        )
        passed[f] = (
            plan(2 * frames + f, ext.at[frames + f, below], ext.at[f, below], later,
                 both(has_next, has_down), both(has_prev, has_down)),
            plan(3 * frames + f, ext.at[frames + f, above], ext.at[f, above], later,
                 both(has_next, has_up), both(has_prev, has_up)),
        )
    onward = plan(4 * frames, ext.at[frames:, own_rows], ext.at[0:frames, own_rows], later, has_next, has_prev)

    def start(made):
        for copy, sends, _ in made:
            pl.when(sends)(copy.start)

    def taken(made):
        for copy, _, takes in made:
            pl.when(takes)(copy.wait_recv)

    def sent(made):
        for copy, sends, _ in made:
            pl.when(sends)(copy.wait_send)

    start(beside[order[0]])
    start([onward])
    for f in order[1:]:
        start(beside[f])

    @pl.when(jnp.logical_not(has_up))
    def _():
        ext[:, above] = jnp.zeros((2 * frames, 2, chans, width), jnp.bfloat16)

    @pl.when(jnp.logical_not(has_down))
    def _():
        ext[:, below] = jnp.zeros((2 * frames, 2, chans, width), jnp.bfloat16)

    @pl.when(jnp.logical_not(has_prev))
    def _():
        ext[0:frames] = jnp.zeros((frames, rows + 4, chans, width), jnp.bfloat16)

    for n, ref in enumerate((small_0, small_1, small_2, small_3)):
        small[n].wait()
        vecs[n] = jnp.broadcast_to(ref[...], (width, chans)).T

    lane = lax.broadcasted_iota(jnp.int32, (chans, width), 1)

    def act(values, gain):
        meansq = jnp.sum(values * values, axis=0, keepdims=True) * (1.0 / chans)
        half = values * lax.rsqrt(meansq + epsilon) * (gain * 0.5)
        return half + half * jnp.tanh(half)

    def place(stack, many, f, p, field):
        shifted = [
            jnp.where(lane == 0, 0.0, pltpu.roll(field, 1, 1)).astype(jnp.bfloat16),
            field.astype(jnp.bfloat16),
            jnp.where(lane == width - 1, 0.0, pltpu.roll(field, width - 1, 1)).astype(jnp.bfloat16),
        ]
        for row in range(many):
            j = p - row
            if 0 <= j < 3:
                for k in range(3):
                    at = f * group + (j * 3 + k) * chans
                    stack[at : at + chans, row * width : (row + 1) * width] = shifted[k]

    def first_at(f, places):
        for p in places:
            place(st_a, rows + 2, f, p, act(ext[f, p].astype(jnp.float32), vecs[0]))

    def split(weights, by_frame):
        for i in range(3):
            by_frame[i * chans : (i + 1) * chans, :] = weights[:, i * group : (i + 1) * group]

    def conv_step(by_frame, stack, sums, count, g):
        low, high = max(0, g - count + 1), min(2, g)
        total = jnp.dot(
            by_frame[low * chans : (high + 1) * chans, :], stack[g * group : (g + 1) * group, :],
            preferred_element_type=jnp.float32,
        )
        whole = None
        for i in range(low, high + 1):
            part = total[(i - low) * chans : (i - low + 1) * chans]
            if i == 2:
                sums[g - i] = part
            elif i == 1:
                sums[g - i] += part
            else:
                whole = sums[g] + part
        return whole

    one = jnp.float32(1.0)
    inside_up = jnp.where(has_up, one, 0.0)
    inside_down = jnp.where(has_down, one, 0.0)
    inside_prev = jnp.where(has_prev, one, 0.0)

    def step(g):
        total = conv_step(by_a, st_a, sum_a, frames + 2, g)
        if total is None:
            return
        for row in range(rows + 2):
            value = act(total[:, row * width : (row + 1) * width] + vecs[1], vecs[2])
            if row == 0:
                value = value * inside_up
            if row == rows + 1:
                value = value * inside_down
            if g < 2:
                value = value * inside_prev
            place(st_b, rows, g, row, value)
        total = conv_step(by_b, st_b, sum_b, frames, g)
        if total is None:
            return
        for row in range(rows):
            value = total[:, row * width : (row + 1) * width] + vecs[3]
            out[0, g, row] = (ext[frames + g, row + 2].astype(jnp.float32) + value).astype(jnp.bfloat16)

    middle = range(2, 2 + rows)
    edges = [0, 1, 2 + rows, 3 + rows]
    for f in order:
        first_at(frames + f, middle)
    load_a.wait()
    split(w_a, by_a)
    load_b.wait()
    split(w_b, by_b)
    for f in order:
        taken(beside[f])
        start(passed[f])
        first_at(frames + f, edges)
        step(frames + f)
    taken([onward])
    for f in order:
        first_at(f, middle)
    for f in order:
        taken(passed[f])
        first_at(f, edges)
        step(f)
    for f in order:
        sent(beside[f])
        sent(passed[f])
    sent([onward])


def local(video, gamma_first, kernel_first, bias_first, gamma_second, kernel_second, bias_second):
    frames, rows, chans, width = video.shape[1:]
    ext = pltpu.VMEM((2 * frames, rows + 4, chans, width), jnp.bfloat16)
    wide = pltpu.VMEM((2 * frames * 9 * chans, (rows + 2) * width), jnp.bfloat16)
    stack = pltpu.VMEM(((frames + 2) * 9 * chans, rows * width), jnp.bfloat16)
    weights = pltpu.VMEM(kernel_first.shape, jnp.bfloat16)
    by_frame = pltpu.VMEM((3 * chans, 9 * chans), jnp.bfloat16)
    vmem = pl.BlockSpec(memory_space=pltpu.VMEM)
    hbm = pl.BlockSpec(memory_space=pl.ANY)
    return pl.pallas_call(
        block_kernel,
        out_shape=pltpu.VMEM(video.shape, jnp.bfloat16),
        in_specs=[hbm] * 7,
        out_specs=vmem,
        scratch_shapes=[
            ext, wide, stack, weights, weights, by_frame, by_frame,
            pltpu.VMEM((frames + 2, chans, (rows + 2) * width), jnp.float32),
            pltpu.VMEM((frames, chans, rows * width), jnp.float32),
            pltpu.VMEM((4, chans, width), jnp.float32),
            *[pltpu.VMEM((1, chans), jnp.float32)] * 4,
            pltpu.SemaphoreType.DMA((7,)),
            pltpu.SemaphoreType.DMA((4 * frames + 1,)),
            pltpu.SemaphoreType.DMA((4 * frames + 1,)),
        ],
        compiler_params=pltpu.CompilerParams(collective_id=0, has_side_effects=True),
        name="residual_block",
    )(
        video, kernel_first, kernel_second, gamma_first[None, :], bias_first[None, :],
        gamma_second[None, :], bias_second[None, :],
    )


def solution(mesh):
    in_specs = (P("groups", "tm", "rows", None, None), P(), P(), P(), P(), P(), P())
    out_specs = P("groups", "tm", "rows", None, None)
    return jax.shard_map(local, mesh=mesh, in_specs=in_specs, out_specs=out_specs, check_vma=False)
```

time: 17 us -> 16.7 us (0.982)
  Pallas kernels: 16.2 us -> 15.8 us
    pallas_call x1, Pallas kernels: 16.2 us -> 15.8 us  [local(): pl.pallas_call(block_kernel, out_shape=pltpu.VMEM(video.shape, jnp.bfloat...]
where the time goes in v3:
time: 16.7 us; the launch traced here: 16.5 us
  Pallas kernels  15.8 us (95%)
  local copies, waits for them, and re-layouts  0.68 us (4%)
    pallas_call x1, Pallas kernels, local(): pl.pallas_call(block_kernel, out_shape=pltpu.VMEM(video.shape, jnp.bfloat...  15.8 us
    unnamed x1, local copies, waits for them, and re-layouts  0.68 us

profile of v3, /device:TPU:0, one launch (start us, length us, event | category | flops | bytes accessed | tf_op | source)
XLA Modules:
  0.0 16.5 jit_solution(5425066835218427514)
XLA Ops:
  0.0 15.8 %residual_block.1 = bf16[1,4,2,96,128]{4,3,2,1,0:T(8,128)(2,1)S(1)} custom-call(bf16[1,4,2,96,128]{4,3,2,1,0:T(8,128)(2,1)} %video.1, bf16[96,2592]{1,0:T(8,128)(2,1)} %k_first.1, bf16[96,2592]{1,0:T(8,128)(2,1)} %k_second.1, f32[1,96]{1,0:T(1,128)} %bitcast.4, f32[1,96]{1,0:T(1,128)} %bitcast.5, f32[1,96]{1,0:T(1,128)} %bitcast.6, f32[1,96]{1,0:T(1,128)} %bitcast.7), custom_call_target="tpu_custom_call" | custom-call | tf_op jit(solution)/shard_map/residual_block/pallas_call | solution.py:220
  15.9 0.7 %copy.9 = bf16[1,4,2,96,128]{4,3,2,1,0:T(8,128)(2,1)} copy(bf16[1,4,2,96,128]{4,3,2,1,0:T(8,128)(2,1)S(1)} %residual_block.1) | data formatting | bytes 393216
